TPU v7x, 256 devices: a whole 4x4x8 slice. The times are simulated.
256 devices in a mesh: rows: 32 (over y_lo, z, core), protos: 8 (over y_hi, x).
Axes of the slice: x: 4, y: 4 (y_hi: 2, y_lo: 2; y = y_hi * 2 + y_lo), z: 8, core: 2. Of those that a mesh axis runs over, the one named last changes fastest.
Arguments:
- teacher: bfloat16 [2048, 256], P('rows')
- students: bfloat16 [8192, 256], P('rows')
- prototypes: bfloat16 [256, 65536], P(None, 'protos')
- pairing: int32 [8192], P('rows'), may hold values from 0 to 63
- layout: int32 [8192], P('rows'), may hold values from 0 to 31, as said below
Outputs:
- grad_students: float32 [8192, 256], P('rows')
- grad_protos: float32 [256, 65536], P('rows', 'protos')
Inputs may be any that keep to these rules, and one draw needn't show every extreme that they name: `layout`: in each aligned block of 256 rows, every value appears exactly 8 times.
All inputs are finite; a program needn't handle non-finite values.
Results may differ from a plain program's by a relative error of at most 0.0003.
The roundings to bfloat16 on the way count: a program that leaves them out, or rounds other values in their place, can miss the bound.
Values may be sent and summed in bfloat16 or wider, within the bound.
A program may use at most 64 MiB of HBM per device.

v0:
```python
import jax
import jax.numpy as jnp
from jax import lax
from jax.sharding import PartitionSpec as P

PROTOS = 65536
ITERS = 2
epsilon = 1e-06
teacher_temp = 0.07
student_temp = 0.1
loss_scale = 16.0


def body(teacher, students, prototypes, pairing, layout):
    row_devices = lax.axis_size("rows")
    tea_count = teacher.shape[0]
    total_teachers = tea_count * row_devices
    local_protos = prototypes.shape[1]
    weights = prototypes.astype(jnp.float32)
    w_norm = jnp.sqrt(jnp.sum(weights * weights, 0) + epsilon)
    w_unit = weights / w_norm
    w_unit_b = w_unit.astype(jnp.bfloat16)
    tea_full = teacher.astype(jnp.float32)
    tea_unit_b = (
        tea_full / jnp.sqrt(jnp.sum(tea_full * tea_full, 1, keepdims=True) + epsilon)
    ).astype(jnp.bfloat16)
    exp_scores = jnp.exp(
        jnp.dot(tea_unit_b, w_unit_b, preferred_element_type=jnp.float32) / teacher_temp
    )
    row_factor = jnp.ones((tea_count,), jnp.float32)
    col_factor = jnp.ones((local_protos,), jnp.float32)
    for sweep in range(ITERS):
        colsum = lax.psum(jnp.sum(exp_scores * row_factor[:, None], 0), "rows")
        col_factor = 1.0 / (PROTOS * colsum)
        rowsum = lax.psum(jnp.sum(exp_scores * col_factor[None, :], 1), "protos")
        row_factor = 1.0 / (total_teachers * rowsum)
    send_order = jnp.argsort(layout, stable=True)
    moved_rows, moved_pairs = (
        lax.all_to_all(students[send_order], "rows", split_axis=0, concat_axis=0, tiled=True),
        lax.all_to_all(pairing[send_order], "rows", split_axis=0, concat_axis=0, tiled=True),
    )
    balanced = total_teachers * exp_scores * row_factor[:, None] * col_factor[None, :]
    target_rows = balanced[moved_pairs]
    stu_full = moved_rows.astype(jnp.float32)
    u_norm = jnp.sqrt(jnp.sum(stu_full * stu_full, 1, keepdims=True) + epsilon)
    stu_unit = stu_full / u_norm
    stu_unit_b = stu_unit.astype(jnp.bfloat16)
    logits = jnp.dot(stu_unit_b, w_unit_b, preferred_element_type=jnp.float32) / student_temp
    exp_logits = jnp.exp(logits)
    denominator = lax.psum(jnp.sum(exp_logits, 1), "protos")
    grad_logits = (
        loss_scale / student_temp * (exp_logits / denominator[:, None] - target_rows)
    ).astype(jnp.bfloat16)
    partial_unit = jnp.einsum(
        "sk,dk->sd", grad_logits, w_unit_b, preferred_element_type=jnp.float32
    )
    grad_unit = lax.psum(partial_unit, "protos")
    grad_rows = (grad_unit - stu_unit * jnp.sum(stu_unit * grad_unit, 1, keepdims=True)) / u_norm
    returned = lax.all_to_all(grad_rows, "rows", split_axis=0, concat_axis=0, tiled=True)
    grad_students = returned[jnp.argsort(send_order)]
    feature_share = prototypes.shape[0] // row_devices
    first_feature = lax.axis_index("rows") * feature_share
    grad_share = lax.psum_scatter(
        jnp.einsum("sd,sk->dk", stu_unit_b, grad_logits, preferred_element_type=jnp.float32),
        "rows",
        scatter_dimension=0,
        tiled=True,
    )
    unit_share = lax.dynamic_slice_in_dim(w_unit, first_feature, feature_share, 0)
    inner = lax.psum(jnp.sum(unit_share * grad_share, 0), "rows")
    grad_protos = (grad_share - unit_share * inner[None, :]) / w_norm
    return (grad_students, grad_protos)


def solution(mesh):
    in_specs = (P("rows", None), P("rows", None), P(None, "protos"), P("rows"), P("rows"))
    out_specs = (P("rows", None), P("rows", "protos"))
    return jax.shard_map(body, mesh=mesh, in_specs=in_specs, out_specs=out_specs, check_vma=False)
```

profile of v0, /device:TPU:16, one launch (start us, length us, event | category | flops | bytes accessed | tf_op | source)
XLA Modules:
  0.0 580.0 jit_solution(10090649880890800840)
XLA Ops:
  8.0 3.9 sort.34
  11.9 2.0 gather_fusion.1
  13.9 0.7 all_to_all.24
  14.6 9.6 %all-to-all-start.1 = ((s32[32,8,1]{1,2,0:T(1,128)}), s32[32,8,1]{1,2,0:T(1,128)S(1)}, u32[]{:S(2)}, u32[]{:S(2)}) async-start(s32[32,8,1]{1,2,0:T(1,128)} %bitcast.2), calls=%async_computation.1 | async-start | bytes 32768 | tf_op jit(solution)/shard_map/all_to_all | solution.py:40
  24.2 3.2 fusion.2
  27.6 1.3 fusion.18
  29.0 108.1 %psum.50 = f32[8192]{0:T(1024)S(1)} all-reduce(f32[8192]{0:T(1024)S(1)} %get-tuple-element.8), channel_id=1, replica_groups=mesh['rows'=32,'protos'=8] {'rows'}, use_global_device_ids=true, to_apply=%region_7.0 | all-reduce | flops 8192 | bytes 65536 | tf_op jit(solution)/shard_map/psum | solution.py:33
  137.3 21.8 %psum.51 = f32[64]{0:T(128)S(1)} all-reduce(f32[64]{0:T(128)S(1)} %multiply_reduce_fusion.2), channel_id=1, replica_groups=mesh['rows'=32,'protos'=8] {'protos'}, use_global_device_ids=true, to_apply=%region_9.0 | all-reduce | flops 64 | bytes 512 | tf_op jit(solution)/shard_map/psum | solution.py:35
  159.4 104.4 %psum.52 = f32[8192]{0:T(1024)S(1)} all-reduce(f32[8192]{0:T(1024)S(1)} %multiply_reduce_fusion.1), channel_id=1, replica_groups=mesh['rows'=32,'protos'=8] {'rows'}, use_global_device_ids=true, to_apply=%region_11.12 | all-reduce | flops 8192 | bytes 65536 | tf_op jit(solution)/shard_map/psum | solution.py:33
  264.0 1.8 gather_fusion
  265.8 3.9 all-to-all-start
  271.1 9.0 %all-to-all-done = bf16[32,8,256]{2,1,0:T(8,128)(2,1)S(1)} async-done(((bf16[32,8,256]{2,1,0:T(8,128)(2,1)}), bf16[32,8,256]{2,1,0:T(8,128)(2,1)S(1)}, u32[]{:S(2)}, u32[]{:S(2)}) %all-to-all-start) | async-done | bytes 131104 | tf_op jit(solution)/shard_map/all_to_all | solution.py:39
  280.3 7.6 %fusion.19 = (f32[256]{0:T(256)S(1)}, f32[256,8192]{1,0:T(8,128)}) fusion(f32[8192]{0:T(1024)S(1)} %add_sqrt_fusion, bf16[256,8192]{1,0:T(8,128)(2,1)} %param.7, f32[256]{0:T(256)S(1)} %sqrt.27, bf16[32,8,256]{2,1,0:T(8,128)(2,1)S(1)} %all-to-all-done), kind=kOutput, calls=%fused_computation.50 | convolution fusion | flops 1084423936 | bytes 12748800 | tf_op jit(solution)/shard_map/dot_general | solution.py:48
  288.0 19.1 %all-reduce = (f32[64]{0:T(128)S(1)}, f32[256]{0:T(256)S(1)}) all-reduce(f32[64]{0:T(128)S(1)} %multiply_reduce_fusion, f32[256]{0:T(256)S(1)} %get-tuple-element.10), channel_id=1, replica_groups=mesh['rows'=32,'protos'=8] {'protos'}, use_global_device_ids=true, to_apply=%region_13.14 | all-reduce | flops 320 | bytes 2560 | tf_op jit(solution)/shard_map/psum | solution.py:35
  307.1 1.9 multiply_multiply_fusion
  309.0 6.2 %gather_fusion.2 = f32[256,8192]{1,0:T(8,128)} fusion(f32[64,8192]{1,0:T(8,128)S(1)} %multiply_multiply_fusion, s32[1024]{0:T(1024)S(1)} %pad_clamp_fusion.1), kind=kCustom, calls=%fused_computation.2 | custom fusion | bytes 16778240 | tf_op jit(solution)/shard_map/gather | solution.py:43
  315.2 6.7 %multiply_convert_fusion = bf16[256,8192]{1,0:T(8,128)(2,1)S(1)} fusion(f32[256,8192]{1,0:T(8,128)} %gather_fusion.2, f32[256,8192]{1,0:T(8,128)} %get-tuple-element.11, f32[256]{0:T(256)S(1)} %get-tuple-element.7), kind=kLoop, calls=%fused_computation.11 | loop fusion | flops 8388608 | bytes 20972544 | tf_op jit(solution)/shard_map/convert_element_type | solution.py:53
  321.9 2.0 copy-done.4
  323.8 2.0 fusion.12
  325.9 6.8 %fusion.7 = f32[256,8192]{1,0:T(8,128)} fusion(bf16[256,8192]{1,0:T(8,128)(2,1)} %copy-done.4, bf16[32,8,256]{2,1,0:T(8,128)(2,1)S(1)} %all-to-all-done, f32[256]{0:T(256)S(1)} %sqrt.27), kind=kOutput, calls=%fused_computation.28 | convolution fusion | flops 1073938432 | bytes 12715008 | tf_op jit(solution)/shard_map/sd,sk->dk/dot_general | solution.py:64
  332.7 76.2 %all-reduce.3.cloned.1.call-done = f32[256,256]{1,0:T(8,128)} async-done(((f32[256,256]{1,0:T(8,128)}), f32[256,256]{1,0:T(8,128)}) %all-reduce.3.cloned.1.call-update) | async-done | bytes 262160 | tf_op jit(solution)/shard_map/psum | solution.py:57
  409.0 1.1 multiply_reduce_fusion.4
  410.1 1.8 divide_bitcast_fusion
  411.9 8.8 %all-to-all-start.2 = ((f32[32,8,256]{2,1,0:T(8,128)}), f32[32,8,256]{2,1,0:T(8,128)S(1)}, u32[]{:S(2)}, u32[]{:S(2)}) async-start(f32[32,8,256]{2,1,0:T(8,128)} %divide_bitcast_fusion), calls=%async_computation.2 | async-start | bytes 524288 | tf_op jit(solution)/shard_map/all_to_all | solution.py:59
  420.7 6.5 %convert_divide_fusion = f32[256,8192]{1,0:T(8,128)} fusion(bf16[256,8192]{1,0:T(8,128)(2,1)} %param.7, f32[8192]{0:T(1024)S(1)} %add_sqrt_fusion), kind=kLoop, calls=%fused_computation.6 | loop fusion | flops 4194304 | bytes 12615680 | tf_op jit(solution)/shard_map/div | solution.py:21
  427.2 3.2 sort.35
  430.4 4.6 all-to-all-done.2
  435.0 1.7 gather_fusion.3
  436.7 28.6 %reduce-scatter.2.cloned.1.call-done = f32[8,8192]{1,0:T(8,128)} async-done(((f32[256,8192]{1,0:T(8,128)}), f32[8,8192]{1,0:T(8,128)}) %reduce-scatter.2.cloned.1.call-update) | async-done | bytes 262160 | tf_op jit(solution)/shard_map/reduce_scatter | solution.py:63
  465.2 1.1 multiply_reduce_fusion.3
  466.4 104.4 %psum.55 = f32[8192]{0:T(1024)S(1)} all-reduce(f32[8192]{0:T(1024)S(1)} %multiply_reduce_fusion.3), channel_id=1, replica_groups=mesh['rows'=32,'protos'=8] {'rows'}, use_global_device_ids=true, to_apply=%region_19.20 | all-reduce | flops 8192 | bytes 65536 | tf_op jit(solution)/shard_map/psum | solution.py:70
  570.8 1.8 subtract_divide_fusion
  (40 shorter events, 2.7 us)
Async XLA Ops:
  8.0 256.0 %copy-start = (bf16[256,256]{1,0:T(8,128)(2,1)S(1)}, bf16[256,256]{1,0:T(8,128)(2,1)}, u32[]{:S(2)}) copy-start(bf16[256,256]{1,0:T(8,128)(2,1)} %param.6) | copy-start | bytes 393220
  8.0 19.4 %copy-start.5 = (bf16[64,256]{1,0:T(8,128)(2,1)S(1)}, bf16[64,256]{1,0:T(8,128)(2,1)}, u32[]{:S(2)}) copy-start(bf16[64,256]{1,0:T(8,128)(2,1)} %param.5) | copy-start | bytes 98308
  14.6 251.2 %all-to-all-start.1 = ((s32[32,8,1]{1,2,0:T(1,128)}), s32[32,8,1]{1,2,0:T(1,128)S(1)}, u32[]{:S(2)}, u32[]{:S(2)}) async-start(s32[32,8,1]{1,2,0:T(1,128)} %bitcast.2), calls=%async_computation.1 | async-start | bytes 32768 | tf_op jit(solution)/shard_map/all_to_all | solution.py:40
  24.2 3.5 copy-start.2
  29.0 259.0 %copy-start.1 = (f32[64,8192]{1,0:T(8,128)}, f32[64,8192]{1,0:T(8,128)S(1)}, u32[]{:S(2)}) copy-start(f32[64,8192]{1,0:T(8,128)S(1)} %get-tuple-element.9) | copy-start | bytes 6291460
  265.8 14.3 %all-to-all-start = ((bf16[32,8,256]{2,1,0:T(8,128)(2,1)}), bf16[32,8,256]{2,1,0:T(8,128)(2,1)S(1)}, u32[]{:S(2)}, u32[]{:S(2)}) async-start(bf16[32,8,256]{2,1,0:T(8,128)(2,1)} %bitcast), calls=%async_computation | async-start | bytes 262144 | tf_op jit(solution)/shard_map/all_to_all | solution.py:39
  269.7 139.2 %all-reduce.3.cloned.1.call-start = ((), (), s32[]{:S(2)}) async-start(), calls=%async_computation.4 | async-start | bytes 524288 | tf_op jit(solution)/shard_map/psum | solution.py:57
  315.2 8.7 %copy-start.3 = (bf16[256,8192]{1,0:T(8,128)(2,1)S(1)}, bf16[256,8192]{1,0:T(8,128)(2,1)}, u32[]{:S(2)}) copy-start(bf16[256,8192]{1,0:T(8,128)(2,1)} %param.7) | copy-start | bytes 12582916
  321.9 2.0 copy-start.4
  325.9 139.4 %reduce-scatter.2.cloned.1.call-start = ((), (), s32[]{:S(2)}) async-start(), calls=%async_computation.5 | async-start | bytes 8650752 | tf_op jit(solution)/shard_map/reduce_scatter | solution.py:63
  411.9 23.1 %all-to-all-start.2 = ((f32[32,8,256]{2,1,0:T(8,128)}), f32[32,8,256]{2,1,0:T(8,128)S(1)}, u32[]{:S(2)}, u32[]{:S(2)}) async-start(f32[32,8,256]{2,1,0:T(8,128)} %divide_bitcast_fusion), calls=%async_computation.2 | async-start | bytes 524288 | tf_op jit(solution)/shard_map/all_to_all | solution.py:59
Sparse Core Ops, SparseCore 0:
  326.0 82.9 all-reduce.2
Sparse Core Ops, SparseCore 1:
  332.8 132.4 reduce-scatter.1
where the time goes:
time: 581 us; the launch traced here: 580 us
  blocking collectives  358 us (62%)
  waiting for transfers between devices  118 us (20%)
  other arithmetic  32.9 us (6%)
  starting transfers between devices  22.3 us (4%)
  matrix products  17.7 us (3%)
  between operations  15.7 us (3%)
  local copies, waits for them, and re-layouts  15.1 us (3%)
    psum x2, blocking collectives, body(): colsum = lax.psum(jnp.sum(exp_scores * row_factor[:, None], 0), 'rows')  212 us
    psum x1, blocking collectives, body(): inner = lax.psum(jnp.sum(unit_share * grad_share, 0), 'rows')  104 us
    psum x1, waiting for transfers between devices, body(): grad_unit = lax.psum(partial_unit, 'protos')  76.2 us
    psum x2, blocking collectives, body(): rowsum = lax.psum(jnp.sum(exp_scores * col_factor[None, :], 1), 'protos')  40.9 us
    reduce_scatter x1, waiting for transfers between devices, body(): lax.psum_scatter(jnp.einsum('sd,sk->dk', stu_unit_b, grad_logits, preferr...  28.6 us
  transfers between devices with their start and end apart: 5, of which 4 were waited for; matrix products, arithmetic and copies ran while one was open for 5% of the time, Pallas kernels for 0%

commit v1 on v0

--- a/solution.py
+++ b/solution.py
@@ -54,7 +54,8 @@
     partial_unit = jnp.einsum(
         "sk,dk->sd", grad_logits, w_unit_b, preferred_element_type=jnp.float32
     )
-    grad_unit = lax.psum(partial_unit, "protos")
+    terms = lax.all_gather(partial_unit, "protos", axis=0, tiled=False)
+    grad_unit = terms.sum(axis=0)
     grad_rows = (grad_unit - stu_unit * jnp.sum(stu_unit * grad_unit, 1, keepdims=True)) / u_norm
     returned = lax.all_to_all(grad_rows, "rows", split_axis=0, concat_axis=0, tiled=True)
     grad_students = returned[jnp.argsort(send_order)]

time: 581 us -> 580 us (level)
    psum x1 -> x0, waiting for transfers between devices: 76.2 us -> none  [body(): grad_unit = lax.psum(partial_unit, 'protos')]
    all_gather x0 -> x1, waiting for transfers between devices: none -> 52.1 us  [body(): terms = lax.all_gather(partial_unit, 'protos', axis=0, tiled=False)]
    reduce_scatter x1, waiting for transfers between devices: 28.6 us -> 50.4 us  [body(): lax.psum_scatter(jnp.einsum('sd,sk->dk', stu_unit_b, grad_logits, preferr...]
where the time goes in v1:
time: 580 us; the launch traced here: 577 us
  blocking collectives  358 us (62%)
  waiting for transfers between devices  116 us (20%)
  other arithmetic  33.7 us (6%)
  starting transfers between devices  20.8 us (4%)
  matrix products  17.7 us (3%)
  between operations  15.7 us (3%)
  local copies, waits for them, and re-layouts  15.1 us (3%)
    psum x2, blocking collectives, body(): colsum = lax.psum(jnp.sum(exp_scores * row_factor[:, None], 0), 'rows')  212 us
    psum x1, blocking collectives, body(): inner = lax.psum(jnp.sum(unit_share * grad_share, 0), 'rows')  105 us
    all_gather x1, waiting for transfers between devices, body(): terms = lax.all_gather(partial_unit, 'protos', axis=0, tiled=False)  52.1 us
    reduce_scatter x1, waiting for transfers between devices, body(): lax.psum_scatter(jnp.einsum('sd,sk->dk', stu_unit_b, grad_logits, preferr...  50.4 us
    psum x2, blocking collectives, body(): rowsum = lax.psum(jnp.sum(exp_scores * col_factor[None, :], 1), 'protos')  40.9 us
  transfers between devices with their start and end apart: 5, of which 4 were waited for; matrix products, arithmetic and copies ran while one was open for 5% of the time, Pallas kernels for 0%

profile of v1, /device:TPU:16, one launch (start us, length us, event | category | flops | bytes accessed | tf_op | source)
XLA Modules:
  0.0 577.2 jit_solution(10180483415915705588)
XLA Ops:
  8.0 3.9 sort.34
  11.9 2.0 gather_fusion.1
  13.9 0.7 all_to_all.22
  14.6 9.6 %all-to-all-start.1 = ((s32[32,8,1]{1,2,0:T(1,128)}), s32[32,8,1]{1,2,0:T(1,128)S(1)}, u32[]{:S(2)}, u32[]{:S(2)}) async-start(s32[32,8,1]{1,2,0:T(1,128)} %bitcast.2), calls=%async_computation.1 | async-start | bytes 32768 | tf_op jit(solution)/shard_map/all_to_all | solution.py:40
  24.2 3.2 fusion.3
  27.6 1.3 fusion.23
  29.0 108.1 %psum.43 = f32[8192]{0:T(1024)S(1)} all-reduce(f32[8192]{0:T(1024)S(1)} %get-tuple-element.8), channel_id=1, replica_groups=mesh['rows'=32,'protos'=8] {'rows'}, use_global_device_ids=true, to_apply=%region_7.0 | all-reduce | flops 8192 | bytes 65536 | tf_op jit(solution)/shard_map/psum | solution.py:33
  137.3 21.8 %psum.44 = f32[64]{0:T(128)S(1)} all-reduce(f32[64]{0:T(128)S(1)} %multiply_reduce_fusion.2), channel_id=1, replica_groups=mesh['rows'=32,'protos'=8] {'protos'}, use_global_device_ids=true, to_apply=%region_9.0 | all-reduce | flops 64 | bytes 512 | tf_op jit(solution)/shard_map/psum | solution.py:35
  159.4 104.4 %psum.45 = f32[8192]{0:T(1024)S(1)} all-reduce(f32[8192]{0:T(1024)S(1)} %multiply_reduce_fusion.1), channel_id=1, replica_groups=mesh['rows'=32,'protos'=8] {'rows'}, use_global_device_ids=true, to_apply=%region_11.12 | all-reduce | flops 8192 | bytes 65536 | tf_op jit(solution)/shard_map/psum | solution.py:33
  264.0 1.8 gather_fusion
  265.8 3.9 all-to-all-start
  271.1 9.0 %all-to-all-done = bf16[32,8,256]{2,1,0:T(8,128)(2,1)S(1)} async-done(((bf16[32,8,256]{2,1,0:T(8,128)(2,1)}), bf16[32,8,256]{2,1,0:T(8,128)(2,1)S(1)}, u32[]{:S(2)}, u32[]{:S(2)}) %all-to-all-start) | async-done | bytes 131104 | tf_op jit(solution)/shard_map/all_to_all | solution.py:39
  280.3 7.6 %fusion.24 = (f32[256]{0:T(256)S(1)}, f32[256,8192]{1,0:T(8,128)}) fusion(f32[8192]{0:T(1024)S(1)} %add_sqrt_fusion, bf16[256,8192]{1,0:T(8,128)(2,1)} %param.7, bf16[32,8,256]{2,1,0:T(8,128)(2,1)S(1)} %all-to-all-done, f32[256]{0:T(256)S(1)} %sqrt.28), kind=kOutput, calls=%fused_computation.55 | convolution fusion | flops 1084423936 | bytes 12748800 | tf_op jit(solution)/shard_map/dot_general | solution.py:48
  288.0 19.1 %all-reduce = (f32[64]{0:T(128)S(1)}, f32[256]{0:T(256)S(1)}) all-reduce(f32[64]{0:T(128)S(1)} %multiply_reduce_fusion, f32[256]{0:T(256)S(1)} %get-tuple-element.10), channel_id=1, replica_groups=mesh['rows'=32,'protos'=8] {'protos'}, use_global_device_ids=true, to_apply=%region_13.14 | all-reduce | flops 320 | bytes 2560 | tf_op jit(solution)/shard_map/psum | solution.py:35
  307.1 1.9 multiply_multiply_fusion
  309.0 6.2 %gather_fusion.2 = f32[256,8192]{1,0:T(8,128)} fusion(f32[64,8192]{1,0:T(8,128)S(1)} %multiply_multiply_fusion, s32[1024]{0:T(1024)S(1)} %pad_clamp_fusion.1), kind=kCustom, calls=%fused_computation.2 | custom fusion | bytes 16778240 | tf_op jit(solution)/shard_map/gather | solution.py:43
  315.2 6.7 %multiply_convert_fusion = bf16[256,8192]{1,0:T(8,128)(2,1)S(1)} fusion(f32[256,8192]{1,0:T(8,128)} %gather_fusion.2, f32[256,8192]{1,0:T(8,128)} %get-tuple-element.11, f32[256]{0:T(256)S(1)} %get-tuple-element.7), kind=kLoop, calls=%fused_computation.12 | loop fusion | flops 8388608 | bytes 20972544 | tf_op jit(solution)/shard_map/convert_element_type | solution.py:53
  321.9 2.0 copy-done.4
  323.8 2.0 fusion.16
  325.9 6.8 %fusion.20 = f32[256,8192]{1,0:T(8,128)} fusion(bf16[256,8192]{1,0:T(8,128)(2,1)} %copy-done.4, bf16[32,8,256]{2,1,0:T(8,128)(2,1)S(1)} %all-to-all-done, f32[256]{0:T(256)S(1)} %sqrt.28), kind=kOutput, calls=%fused_computation.53 | convolution fusion | flops 1073938432 | bytes 12715008 | tf_op jit(solution)/shard_map/sd,sk->dk/dot_general | solution.py:65
  332.7 52.1 %all-gather.3.cloned.1.call-done = f32[2048,256]{1,0:T(8,128)} async-done(((f32[256,256]{1,0:T(8,128)}), f32[2048,256]{1,0:T(8,128)}) %all-gather.3.cloned.1.call-update) | async-done | bytes 2097168 | tf_op jit(solution)/shard_map/all_gather | solution.py:57
  384.9 1.8 reduce_sum.109
  386.7 2.0 fusion.6
  388.6 7.3 %all-to-all-start.2 = ((f32[32,8,256]{2,1,0:T(8,128)}), f32[32,8,256]{2,1,0:T(8,128)S(1)}, u32[]{:S(2)}, u32[]{:S(2)}) async-start(f32[32,8,256]{2,1,0:T(8,128)} %fusion.6), calls=%async_computation.2 | async-start | bytes 524288 | tf_op jit(solution)/shard_map/all_to_all | solution.py:60
  396.0 6.5 %convert_divide_fusion = f32[256,8192]{1,0:T(8,128)} fusion(bf16[256,8192]{1,0:T(8,128)(2,1)} %param.7, f32[8192]{0:T(1024)S(1)} %add_sqrt_fusion), kind=kLoop, calls=%fused_computation.7 | loop fusion | flops 4194304 | bytes 12615680 | tf_op jit(solution)/shard_map/div | solution.py:21
  402.4 3.2 sort.35
  405.6 4.4 all-to-all-done.2
  410.0 1.7 gather_fusion.3
  411.6 50.4 %reduce-scatter.2.cloned.1.call-done = f32[8,8192]{1,0:T(8,128)} async-done(((f32[256,8192]{1,0:T(8,128)}), f32[8,8192]{1,0:T(8,128)}) %reduce-scatter.2.cloned.1.call-update) | async-done | bytes 262160 | tf_op jit(solution)/shard_map/reduce_scatter | solution.py:64
  462.0 1.1 multiply_reduce_fusion.3
  463.1 104.9 %psum.47 = f32[8192]{0:T(1024)S(1)} all-reduce(f32[8192]{0:T(1024)S(1)} %multiply_reduce_fusion.3), channel_id=1, replica_groups=mesh['rows'=32,'protos'=8] {'rows'}, use_global_device_ids=true, to_apply=%region_19.20 | all-reduce | flops 8192 | bytes 65536 | tf_op jit(solution)/shard_map/psum | solution.py:71
  568.0 1.8 subtract_divide_fusion
  (40 shorter events, 2.7 us)
Async XLA Ops:
  8.0 256.0 %copy-start = (bf16[256,256]{1,0:T(8,128)(2,1)S(1)}, bf16[256,256]{1,0:T(8,128)(2,1)}, u32[]{:S(2)}) copy-start(bf16[256,256]{1,0:T(8,128)(2,1)} %param.6) | copy-start | bytes 393220
  8.0 19.4 %copy-start.5 = (bf16[64,256]{1,0:T(8,128)(2,1)S(1)}, bf16[64,256]{1,0:T(8,128)(2,1)}, u32[]{:S(2)}) copy-start(bf16[64,256]{1,0:T(8,128)(2,1)} %param.5) | copy-start | bytes 98308
  14.6 251.2 %all-to-all-start.1 = ((s32[32,8,1]{1,2,0:T(1,128)}), s32[32,8,1]{1,2,0:T(1,128)S(1)}, u32[]{:S(2)}, u32[]{:S(2)}) async-start(s32[32,8,1]{1,2,0:T(1,128)} %bitcast.2), calls=%async_computation.1 | async-start | bytes 32768 | tf_op jit(solution)/shard_map/all_to_all | solution.py:40
  24.2 3.5 copy-start.2
  29.0 259.0 %copy-start.1 = (f32[64,8192]{1,0:T(8,128)}, f32[64,8192]{1,0:T(8,128)S(1)}, u32[]{:S(2)}) copy-start(f32[64,8192]{1,0:T(8,128)S(1)} %get-tuple-element.9) | copy-start | bytes 6291460
  265.8 14.3 %all-to-all-start = ((bf16[32,8,256]{2,1,0:T(8,128)(2,1)}), bf16[32,8,256]{2,1,0:T(8,128)(2,1)S(1)}, u32[]{:S(2)}, u32[]{:S(2)}) async-start(bf16[32,8,256]{2,1,0:T(8,128)(2,1)} %bitcast), calls=%async_computation | async-start | bytes 262144 | tf_op jit(solution)/shard_map/all_to_all | solution.py:39
  269.7 115.1 %all-gather.3.cloned.1.call-start = ((), (), s32[]{:S(2)}) async-start(), calls=%async_computation.5 | async-start | bytes 2359296 | tf_op jit(solution)/shard_map/all_gather | solution.py:57
  315.2 8.7 %copy-start.3 = (bf16[256,8192]{1,0:T(8,128)(2,1)S(1)}, bf16[256,8192]{1,0:T(8,128)(2,1)}, u32[]{:S(2)}) copy-start(bf16[256,8192]{1,0:T(8,128)(2,1)} %param.7) | copy-start | bytes 12582916
  321.9 2.0 copy-start.4
  325.9 136.1 %reduce-scatter.2.cloned.1.call-start = ((), (), s32[]{:S(2)}) async-start(), calls=%async_computation.4 | async-start | bytes 8650752 | tf_op jit(solution)/shard_map/reduce_scatter | solution.py:64
  388.6 21.3 %all-to-all-start.2 = ((f32[32,8,256]{2,1,0:T(8,128)}), f32[32,8,256]{2,1,0:T(8,128)S(1)}, u32[]{:S(2)}, u32[]{:S(2)}) async-start(f32[32,8,256]{2,1,0:T(8,128)} %fusion.6), calls=%async_computation.2 | async-start | bytes 524288 | tf_op jit(solution)/shard_map/all_to_all | solution.py:60
Sparse Core Ops, SparseCore 0:
  326.0 58.8 all-gather.2
Sparse Core Ops, SparseCore 1:
  332.8 129.1 reduce-scatter.1
